TPU v7x, 32 devices: a whole 2x2x4 slice. The times are simulated.
32 devices in a mesh: table: 8 (over z, x), replica: 4 (over y, core).
Axes of the slice: x: 2, y: 2, z: 4, core: 2. Of those that a mesh axis runs over, the one named last changes fastest.
Arguments:
- emb_table: bfloat16 [8192, 128], P('table'), may hold values from -3 to 3
- cross_up: bfloat16 [256, 3456], replicated, may hold values from -0.375 to 0.375
- cross_down: bfloat16 [256, 3456], replicated, may hold values from -0.109375 to 0.109375
- cross_bias: float32 [3456], replicated, may hold values from -3 to 3
- out_weight: float32 [3456], replicated, may hold values from -0.109375 to 0.109375
- bottom_weight: float32 [13, 128], replicated, may hold values from -1.75 to 1.75
- bottom_bias: float32 [128], replicated, may hold values from -3 to 3
- dense_in: float32 [4096, 13], P(('table', 'replica')), may hold values from -6 to 6
- labels: int32 [4096], P(('table', 'replica')), may hold values from 0 to 1
- lookup_ids: int32 [4096, 26, 4], P(('table', 'replica')), may hold values from 0 to 767
- bag_weight: float32 [4096, 26, 4], P(('table', 'replica')), may hold values from 0.25 to 1
- bag_length: int32 [4096, 26], P(('table', 'replica')), may hold values from 1 to 4
- want_blocks: int32 [8, 4, 8, 1], P('table', 'replica'), may hold values from 0 to 31
- hot_blocks: int32 [8, 2], P('table'), may hold values from 0 to 31
- hot_count: int32 [8], P('table'), may hold values from 1 to 2, as said below
Outputs:
- up_grad: float32 [256, 3456], P(('table', 'replica'))
- down_grad: float32 [256, 3456], P(('table', 'replica'))
- table_grad: float32 [8192, 128], P(('table', 'replica'))
Inputs may be any that keep to these rules, and one draw needn't show every extreme that they name: `hot_count`: each owner has 1 to 2 live hot slots, and some owner has 2.
All inputs are finite; a program needn't handle non-finite values.
Results may differ from a plain program's by a relative error of at most 0.0053.
Values may be sent and summed in bfloat16 or wider, within the bound.
A program may use at most 64 MiB of HBM per device.

v0:
```python
import jax
import jax.numpy as jnp
from jax import lax
from jax.sharding import PartitionSpec as P

EMB = 128
BLOCK = 32


def local_step(
    cached_rows,
    dense_dev,
    labels_dev,
    ids_dev,
    weight_dev,
    length_dev,
    cross_up,
    cross_down,
    cross_bias,
    out_weight,
    bottom_weight,
    bottom_bias,
):
    batch = ids_dev.shape[0]
    width = cached_rows.shape[1]
    gathered = cached_rows[ids_dev].astype(jnp.float32)
    slots = jnp.arange(ids_dev.shape[2], dtype=jnp.int32)
    bag_coef = jnp.where(
        slots[None, None, :] < length_dev[:, :, None], weight_dev, jnp.zeros((), jnp.float32)
    )
    pooled = jnp.sum(bag_coef[..., None] * gathered, axis=2)
    bottom = jax.nn.relu(
        jnp.dot(dense_dev, bottom_weight, precision=lax.Precision.HIGHEST) + bottom_bias
    )
    cross_base = jnp.concatenate([bottom, pooled.reshape(batch, -1)], 1).astype(jnp.bfloat16)
    low_rank = lax.dot_general(
        cross_base, cross_down, (((1,), (1,)), ((), ())), preferred_element_type=jnp.float32
    ).astype(jnp.bfloat16)
    cross_gate = jnp.dot(low_rank, cross_up, preferred_element_type=jnp.float32) + cross_bias
    base_wide = cross_base.astype(jnp.float32)
    crossed = base_wide * cross_gate + base_wide
    logits = jnp.dot(crossed, out_weight, precision=lax.Precision.HIGHEST)
    logit_grad = jax.nn.sigmoid(logits) - labels_dev.astype(jnp.float32)
    grad_crossed = logit_grad[:, None] * out_weight[None, :]
    g_cross = (grad_crossed * base_wide).astype(jnp.bfloat16)
    g_low = lax.dot_general(
        g_cross, cross_up, (((1,), (1,)), ((), ())), preferred_element_type=jnp.float32
    ).astype(jnp.bfloat16)
    up_part = lax.dot_general(
        low_rank, g_cross, (((0,), (0,)), ((), ())), preferred_element_type=jnp.float32
    )
    down_part = lax.dot_general(
        g_low, cross_base, (((0,), (0,)), ((), ())), preferred_element_type=jnp.float32
    )
    grad_base = grad_crossed * (cross_gate + 1.0) + jnp.dot(
        g_low, cross_down, preferred_element_type=jnp.float32
    )
    grad_pooled = grad_base[:, width:].reshape(batch, -1, width)
    contrib = bag_coef[..., None] * grad_pooled[:, :, None, :]
    cache_grad = (
        jnp.zeros(cached_rows.shape, jnp.float32)
        .at[ids_dev.reshape(-1)]
        .add(contrib.reshape(-1, width))
    )
    return (up_part, down_part, cache_grad)


def local(
    emb_table,
    cross_up,
    cross_down,
    cross_bias,
    out_weight,
    bottom_weight,
    bottom_bias,
    dense_in,
    labels,
    lookup_ids,
    bag_weight,
    bag_length,
    want_blocks,
    hot_blocks,
    hot_count,
):
    owners = lax.axis_size("table")
    blocks = emb_table.reshape(-1, BLOCK, EMB)
    block_total = blocks.shape[0]
    wanted = want_blocks.reshape(owners, want_blocks.shape[3])
    asked_for = lax.all_to_all(wanted, "table", split_axis=0, concat_axis=0, tiled=True)
    served = blocks[asked_for]
    cold_rows = lax.all_to_all(served, "table", split_axis=0, concat_axis=0, tiled=True)
    slot_count = hot_blocks.shape[1]
    alive = jnp.arange(slot_count, dtype=jnp.int32) < hot_count[0]
    own_hot = jnp.where(alive[:, None, None], blocks[hot_blocks[0]], jnp.zeros((), jnp.bfloat16))
    hot_rows = lax.all_gather(own_hot[:, None], "table", axis=1, tiled=True)
    cold_count = cold_rows.shape[0] * cold_rows.shape[1] * BLOCK
    cached_rows = jnp.concatenate([cold_rows.reshape(-1, EMB), hot_rows.reshape(-1, EMB)], 0)
    up_part, down_part, cache_grad = local_step(
        cached_rows,
        dense_in,
        labels,
        lookup_ids,
        bag_weight,
        bag_length,
        cross_up,
        cross_down,
        cross_bias,
        out_weight,
        bottom_weight,
        bottom_bias,
    )
    cold_grad = cache_grad[:cold_count].reshape(cold_rows.shape).astype(jnp.bfloat16)
    returned = lax.all_to_all(cold_grad, "table", split_axis=0, concat_axis=0, tiled=True)
    hot_grad = cache_grad[cold_count:].reshape(hot_rows.shape)
    hot_sums = lax.psum_scatter(hot_grad, "table", scatter_dimension=1, tiled=True)[:, 0]
    block_ids = jnp.arange(block_total, dtype=jnp.int32)
    cold_pick = (asked_for.reshape(-1)[:, None] == block_ids[None, :]).astype(jnp.bfloat16)
    hot_pick = ((hot_blocks[0][:, None] == block_ids[None, :]) & alive[:, None]).astype(jnp.float32)
    block_grad = lax.dot_general(
        cold_pick,
        returned.reshape(cold_pick.shape[0], -1),
        (((0,), (0,)), ((), ())),
        preferred_element_type=jnp.float32,
    )
    block_grad = block_grad + lax.dot_general(
        hot_pick,
        hot_sums.reshape(slot_count, -1),
        (((0,), (0,)), ((), ())),
        precision=lax.Precision.HIGHEST,
    )
    table_grad = lax.psum_scatter(
        block_grad.reshape(-1, EMB), "replica", scatter_dimension=0, tiled=True
    )
    up_grad, down_grad = (
        lax.psum_scatter(up_part, ("table", "replica"), scatter_dimension=0, tiled=True),
        lax.psum_scatter(down_part, ("table", "replica"), scatter_dimension=0, tiled=True),
    )
    return (up_grad, down_grad, table_grad)


def solution(mesh):
    placed = (
        P("table", None),
        P(),
        P(),
        P(),
        P(),
        P(),
        P(),
        P(("table", "replica"), None),
        P(("table", "replica")),
        P(("table", "replica"), None, None),
        P(("table", "replica"), None, None),
        P(("table", "replica"), None),
        P("table", "replica", None, None),
        P("table", None),
        P("table"),
    )
    return jax.shard_map(
        local,
        mesh=mesh,
        in_specs=placed,
        out_specs=(
            P(("table", "replica"), None),
            P(("table", "replica"), None),
            P(("table", "replica"), None),
        ),
        check_vma=False,
    )
```

profile of v0, /device:TPU:0, one launch (start us, length us, event | category | flops | bytes accessed | tf_op | source)
XLA Modules:
  0.0 504.9 jit_solution(10826503403395915220)
XLA Ops:
  7.2 1.5 copy.49
  8.6 7.3 %all-to-all-start = ((s32[8,1,1]{2,1,0:T(1,128)}), s32[8,1,1]{2,1,0:T(1,128)S(1)}, u32[]{:S(2)}, u32[]{:S(2)}) async-start(s32[8,1,1]{2,1,0:T(1,128)} %copy.49), calls=%async_computation | async-start | bytes 8192 | tf_op jit(solution)/shard_map/all_to_all | solution.py:89
  15.9 0.8 compare_select_fusion.1
  16.8 3.7 copy.55
  21.1 2.9 copy.50
  24.0 2.1 reshape.167
  26.1 2.2 reshape.145
  28.3 0.7 compare_select_fusion
  29.0 0.3 fusion.7
  29.3 1.5 gather_fusion.1
  30.9 0.4 fusion.33
  31.2 2.1 gather_fusion
  33.4 6.0 %all-to-all-start.1 = ((bf16[8,1,32,128]{3,2,1,0:T(8,128)(2,1)}), bf16[8,1,32,128]{3,2,1,0:T(8,128)(2,1)S(1)}, u32[]{:S(2)}, u32[]{:S(2)}) async-start(bf16[8,1,32,128]{3,2,1,0:T(8,128)(2,1)} %bitcast.2), calls=%async_computation.1 | async-start | bytes 131072 | tf_op jit(solution)/shard_map/all_to_all | solution.py:91
  39.5 2.9 copy.48
  42.6 2.7 mul.57
  45.3 31.3 %all_gather.3 = bf16[2,8,32,128]{3,2,1,0:T(8,128)(2,1)S(1)} all-gather(bf16[2,1,32,128]{3,2,1,0:T(8,128)(2,1)S(1)} %bitcast_select_fusion), channel_id=1, replica_groups=mesh['table'=8,'replica'=4] {'table'}, dimensions={1}, use_global_device_ids=true | all-gather | bytes 147456 | tf_op jit(solution)/shard_map/all_gather | solution.py:95
  76.6 46.8 %gather_fusion.2 = bf16[13312,128]{1,0:T(8,128)(2,1)} fusion(bf16[768,128]{1,0:T(8,128)(2,1)S(1)} %pad_maximum_fusion.1, s32[13312]{0:T(1024)S(1)} %broadcast_clamp_fusion), kind=kCustom, calls=%fused_computation.2 | custom fusion | bytes 6868992 | tf_op jit(solution)/shard_map/gather | solution.py:26
  123.3 6.5 %fusion = bf16[128,26,128]{2,1,0:T(8,128)(2,1)S(1)} fusion(bf16[128,26,4,128]{3,2,1,0:T(4,128)(2,1)} %bitcast.64, f32[128,26,4]{2,1,0:T(8,128)} %copy.48), kind=kLoop, calls=%fused_computation.5 | loop fusion | flops 4685824 | bytes 4313088 | tf_op jit(solution)/shard_map/reduce_sum | solution.py:31
  129.9 0.3 copy.72
  130.2 0.6 copy.52
  130.9 0.6 copy.54
  131.5 2.2 convolution_convert_fusion.1
  133.7 0.4 convolution_add_fusion
  134.1 0.2 copy-done.8
  134.4 1.6 fusion.13
  136.0 0.8 convolution_convert_fusion
  136.7 0.2 broadcast_multiply_fusion
  136.9 2.4 fusion.15
  139.4 0.4 fusion.34
  139.8 1.4 slice_add_fusion
  141.2 2.7 copy.57
  143.9 3.1 copy.58
  147.0 5.7 %mul.61 = f32[128,26,4,128]{3,2,1,0:T(4,128)} broadcast(f32[128,26,128]{2,1,0:T(8,128)} %copy.58), dimensions={0,1,3} | broadcast | bytes 8519680 | tf_op jit(solution)/shard_map/mul | solution.py:59
  152.7 78.3 %scatter_custom_fusion = f32[768,128]{1,0:T(8,128)S(1)} fusion(s32[13312]{0:T(1024)} %bitcast.71, f32[13312,128]{1,0:T(8,128)} %bitcast.63, f32[13312]{0:T(1024)S(1)} %copy-done.2, f32[]{:T(128)} %constant.6.clone.1), kind=kCustom, calls=%fused_computation.6 | custom fusion | flops 3407872 | bytes 7262720 | tf_op jit(solution)/shard_map/scatter-add | solution.py:63
  231.1 0.7 slice.23
  231.9 2.5 fusion.32
  234.4 0.6 slice.32
  235.0 5.4 %all-to-all-start.2 = ((bf16[8,1,32,128]{3,2,1,0:T(8,128)(2,1)}), bf16[8,1,32,128]{3,2,1,0:T(8,128)(2,1)S(1)}, u32[]{:S(2)}, u32[]{:S(2)}) async-start(bf16[8,1,32,128]{3,2,1,0:T(8,128)(2,1)} %bitcast.15), calls=%async_computation.2 | async-start | bytes 131072 | tf_op jit(solution)/shard_map/all_to_all | solution.py:113
  240.4 0.6 dynamic-slice.2
  241.0 6.4 %all-to-all-done.2 = bf16[8,1,32,128]{3,2,1,0:T(8,128)(2,1)S(1)} async-done(((bf16[8,1,32,128]{3,2,1,0:T(8,128)(2,1)}), bf16[8,1,32,128]{3,2,1,0:T(8,128)(2,1)S(1)}, u32[]{:S(2)}, u32[]{:S(2)}) %all-to-all-start.2) | async-done | bytes 65568 | tf_op jit(solution)/shard_map/all_to_all | solution.py:113
  247.4 0.3 fusion.18
  247.8 56.1 %all-reduce.7.cloned.1.call-done = f32[2,8,32,128]{3,2,1,0:T(8,128)} async-done(((f32[2,8,32,128]{3,2,1,0:T(8,128)}), f32[2,8,32,128]{3,2,1,0:T(8,128)}) %all-reduce.7.cloned.1.call-update) | async-done | bytes 262160
  303.9 1.4 dynamic-slice_bitcast_fusion
  305.3 0.5 convolution_add_fusion.1
  305.8 0.9 reshape.148
  306.7 166.9 %all-reduce.9.cloned.1.call-done = (f32[256,3456]{1,0:T(8,128)}, f32[256,3456]{1,0:T(8,128)}) async-done(((f32[256,3456]{1,0:T(8,128)}, f32[256,3456]{1,0:T(8,128)}), (f32[256,3456]{1,0:T(8,128)}, f32[256,3456]{1,0:T(8,128)})) %all-reduce.9.cloned.1.call-update) | async-done | bytes 7077904
  473.6 1.6 constant_dynamic-slice_fusion
  475.2 23.2 %reduce-scatter.5.cloned.1.call-done = f32[256,128]{1,0:T(8,128)} async-done(((f32[1024,128]{1,0:T(8,128)}), f32[256,128]{1,0:T(8,128)}) %reduce-scatter.5.cloned.1.call-update) | async-done | bytes 131088 | tf_op jit(solution)/shard_map/reduce_scatter | solution.py:131
  (43 shorter events, 0.5 us)
Async XLA Ops:
  7.2 126.5 %copy-start = (bf16[256,3456]{1,0:T(8,128)(2,1)S(1)}, bf16[256,3456]{1,0:T(8,128)(2,1)}, u32[]{:S(2)}) copy-start(bf16[256,3456]{1,0:T(8,128)(2,1)} %param.16) | copy-start | bytes 5308420
  7.2 13.2 %copy-start.7 = (s32[1,2]{1,0:T(1,128)S(1)}, s32[1,2]{1,0:T(1,128)}, u32[]{:S(2)}) copy-start(s32[1,2]{1,0:T(1,128)} %param.28) | copy-start | bytes 28
  8.6 22.2 %all-to-all-start = ((s32[8,1,1]{2,1,0:T(1,128)}), s32[8,1,1]{2,1,0:T(1,128)S(1)}, u32[]{:S(2)}, u32[]{:S(2)}) async-start(s32[8,1,1]{2,1,0:T(1,128)} %copy.49), calls=%async_computation | async-start | bytes 8192 | tf_op jit(solution)/shard_map/all_to_all | solution.py:89
  24.0 5.0 copy-start.4
  24.0 5.0 copy-start.6
  26.0 3.0 copy-start.9
  26.1 3.0 copy-start.10
  26.1 3.0 copy-start.11
  28.3 14.2 %copy-start.3 = (f32[3456]{0:T(1024)S(1)}, f32[3456]{0:T(1024)}, u32[]{:S(2)}) copy-start(f32[3456]{0:T(1024)} %param.19) | copy-start | bytes 41476
  33.4 43.2 %all-to-all-start.1 = ((bf16[8,1,32,128]{3,2,1,0:T(8,128)(2,1)}), bf16[8,1,32,128]{3,2,1,0:T(8,128)(2,1)S(1)}, u32[]{:S(2)}, u32[]{:S(2)}) async-start(bf16[8,1,32,128]{3,2,1,0:T(8,128)(2,1)} %bitcast.2), calls=%async_computation.1 | async-start | bytes 131072 | tf_op jit(solution)/shard_map/all_to_all | solution.py:91
  39.4 264.5 %all-reduce.7.cloned.1.call-start = ((), (), s32[]{:S(2)}) async-start(), calls=%async_computation.5 | async-start | bytes 524288
  131.5 2.2 copy-start.5
  133.7 0.7 copy-start.8
  136.9 2.5 copy-start.1
  147.0 5.7 %copy-start.2 = (f32[13312]{0:T(1024)S(1)}, f32[13312]{0:T(1024)}, u32[]{:S(2)}) copy-start(f32[13312]{0:T(1024)} %mul.57) | copy-start | bytes 159748
  231.8 241.8 %all-reduce.9.cloned.1.call-start = ((), (), s32[]{:S(2)}) async-start(), calls=%async_computation.6 | async-start | bytes 14155776
  234.4 6.1 %copy-start.12 = (u32[32]{0:T(128)S(1)}, u32[32]{0:T(128)}, u32[]{:S(2)}) copy-start(u32[32]{0:T(128)} %constant.32) | copy-start | bytes 388
  235.0 12.4 %all-to-all-start.2 = ((bf16[8,1,32,128]{3,2,1,0:T(8,128)(2,1)}), bf16[8,1,32,128]{3,2,1,0:T(8,128)(2,1)S(1)}, u32[]{:S(2)}, u32[]{:S(2)}) async-start(bf16[8,1,32,128]{3,2,1,0:T(8,128)(2,1)} %bitcast.15), calls=%async_computation.2 | async-start | bytes 131072 | tf_op jit(solution)/shard_map/all_to_all | solution.py:113
  240.4 258.0 %reduce-scatter.5.cloned.1.call-start = ((), (), s32[]{:S(2)}) async-start(), calls=%async_computation.4 | async-start | bytes 655360 | tf_op jit(solution)/shard_map/reduce_scatter | solution.py:131
Sparse Core Ops, SparseCore 0:
  231.9 71.8 all-reduce.6
  309.9 163.6 all-reduce.8
  476.6 21.6 reduce-scatter.4
where the time goes:
time: 506 us; the launch traced here: 505 us
  waiting for transfers between devices  253 us (50%)
  other arithmetic  88.5 us (17%)
  local copies, waits for them, and re-layouts  87.6 us (17%)
  blocking collectives  31.3 us (6%)
  starting transfers between devices  18.7 us (4%)
  between operations  14.7 us (3%)
  matrix products  11.4 us (2%)
    unnamed x5, waiting for transfers between devices  223 us
    scatter-add x1, other arithmetic, local_step(): cache_grad = jnp.zeros(cached_rows.shape, jnp.float32).at[ids_dev.reshape...  78.3 us
    gather x1, local copies, waits for them, and re-layouts, local_step(): gathered = cached_rows[ids_dev].astype(jnp.float32)  46.8 us
    all_gather x1, blocking collectives, local(): hot_rows = lax.all_gather(own_hot[:, None], 'table', axis=1, tiled=True)  31.3 us
    reduce_scatter x1, waiting for transfers between devices, local(): lax.psum_scatter(block_grad.reshape(-1, EMB), 'replica', scatter_dimensio...  23.2 us
  transfers between devices with their start and end apart: 6, of which 4 were waited for; matrix products, arithmetic and copies ran while one was open for 6% of the time, Pallas kernels for 0%

commit v1 on v0

--- a/solution.py
+++ b/solution.py
@@ -1,10 +1,483 @@
+import functools
+
 import jax
 import jax.numpy as jnp
 from jax import lax
+from jax.experimental import pallas as pl
+from jax.experimental.pallas import tpu as pltpu
 from jax.sharding import PartitionSpec as P
 
 EMB = 128
 BLOCK = 32
+LANES = 128
+SUBLANES = 8
+MESH = pl.DeviceIdType.MESH
+F32 = jnp.float32
+BF16 = jnp.bfloat16
+
+
+def vmem(n):
+    return [pl.BlockSpec(memory_space=pltpu.VMEM)] * n
+
+
+def pick_rows(ids, emb_ref):
+    total = emb_ref.shape[0]
+    tiles = total // LANES
+    row = lax.broadcasted_iota(jnp.int32, (BLOCK, LANES), 0)
+    lane = lax.broadcasted_iota(jnp.int32, (BLOCK, LANES), 1)
+    parts = []
+    for block in ids:
+        want = block * BLOCK + row
+        parts.append(
+            jnp.concatenate(
+                [jnp.where(want == lane + LANES * c, 1.0, 0.0) for c in range(tiles)], axis=1
+            )
+        )
+    pick = jnp.concatenate(parts, axis=0).astype(BF16)
+    return jnp.dot(pick, emb_ref[...], preferred_element_type=F32).astype(BF16)
+
+
+def fetch_kernel(
+    owners, want_ref, hot_ref, emb_ref, cold_ref, hot_out, ask_ref, serve, own_hot,
+    id_send, id_recv, hs_send, hs_recv, cs_send, cs_recv,
+):
+    me = lax.axis_index("table")
+    slots = hot_ref.shape[0]
+    wants = want_ref.shape[1]
+
+    def peer(k):
+        return lax.rem(me + k, owners)
+
+    def copy(src, dst, send, recv, k):
+        return pltpu.make_async_remote_copy(
+            src_ref=src, dst_ref=dst, send_sem=send.at[k], recv_sem=recv.at[k],
+            device_id=(peer(k), lax.axis_index("replica")), device_id_type=MESH,
+        )
+
+    barrier = pltpu.get_barrier_semaphore()
+    for k in range(1, owners):
+        pl.semaphore_signal(
+            barrier, inc=1, device_id=(peer(k), lax.axis_index("replica")), device_id_type=MESH
+        )
+    ask_ref[me] = want_ref[me]
+    hot = pick_rows([hot_ref[s, 0:1, :] for s in range(slots)], emb_ref)
+    hot = hot.reshape(slots, BLOCK, EMB)
+    own_hot[...] = hot
+    hot_out[:, me] = hot
+    pl.semaphore_wait(barrier, owners - 1)
+
+    id_copies = [
+        copy(want_ref.at[peer(k)], ask_ref.at[me], id_send, id_recv, k) for k in range(1, owners)
+    ]
+    for c in id_copies:
+        c.start()
+    hot_copies = [
+        copy(own_hot, hot_out.at[:, me], hs_send, hs_recv, k) for k in range(1, owners)
+    ]
+    for c in hot_copies:
+        c.start()
+    for c in id_copies:
+        c.wait()
+    asked = [ask_ref[p, w, 0:1, :] for p in range(owners) for w in range(wants)]
+    serve[...] = pick_rows(asked, emb_ref).reshape(owners, wants, BLOCK, EMB)
+    cold_copies = [
+        copy(serve.at[peer(k)], cold_ref.at[me], cs_send, cs_recv, k) for k in range(1, owners)
+    ]
+    for c in cold_copies:
+        c.start()
+    cold_ref[me] = serve[me]
+    for c in hot_copies + cold_copies:
+        c.wait()
+
+
+def fetch(want, hot_ids, emb, owners):
+    wants, slots = want.shape[1], hot_ids.shape[0]
+    sems = [pltpu.SemaphoreType.DMA((owners,))] * 6
+    return pl.pallas_call(
+        functools.partial(fetch_kernel, owners),
+        out_shape=[
+            jax.ShapeDtypeStruct((owners, wants, BLOCK, EMB), BF16),
+            jax.ShapeDtypeStruct((slots, owners, BLOCK, EMB), BF16),
+            jax.ShapeDtypeStruct(want.shape, jnp.int32),
+        ],
+        in_specs=vmem(3),
+        out_specs=vmem(3),
+        scratch_shapes=[
+            pltpu.VMEM((owners, wants, BLOCK, EMB), BF16),
+            pltpu.VMEM((slots, BLOCK, EMB), BF16),
+        ] + sems,
+        compiler_params=pltpu.CompilerParams(collective_id=0, has_side_effects=True),
+        name="fetch",
+    )(want, hot_ids, emb)
+
+
+def compute_kernel(
+    plan, bag,
+    cold_ref, hot_ref, ids_ref, weight_ref, length_ref, dense_ref, label_ref, up_ref, down_ref, bias_ref,
+    outw_ref, bw_ref, bb_ref,
+    acc_ref, cold_grad, hot_grad,
+    pick, rows, base, gate, gcross, grad, ids_cols, coef_cols, turn,
+):
+    feats, batch, cache = pick.shape
+    cold = cold_ref.shape[0]
+    width = base.shape[1]
+    group = 16
+    rows[:cold] = cold_ref[...]
+    rows[cold:] = hot_ref[...]
+
+    turn[...] = jnp.zeros_like(turn)
+    for f in range(feats):
+        turn[f * bag:(f + 1) * bag, :] = ids_ref[f].astype(F32)
+    ids_cols[...] = turn[...].T
+    spot = lax.broadcasted_iota(jnp.int32, (bag, batch), 0)
+    for f in range(feats):
+        live = spot < length_ref[f:f + 1, :]
+        turn[f * bag:(f + 1) * bag, :] = jnp.where(live, weight_ref[f], 0.0)
+    coef_cols[...] = turn[...].T
+
+    @pl.loop(0, batch // group)
+    def _(g):
+        at = pl.ds(pl.multiple_of(g * group, group), group)
+        ids = ids_cols[at, :]
+        coef = coef_cols[at, :]
+        lane = lax.broadcasted_iota(jnp.int32, (group, cache), 1).astype(F32)
+        for f in range(feats):
+            total = None
+            for l in range(bag):
+                j = f * bag + l
+                term = jnp.where(ids[:, j:j + 1] == lane, coef[:, j:j + 1], 0.0)
+                total = term if total is None else total + term
+            pick[f, at, :] = total.astype(BF16)
+
+    bottom = jnp.zeros((batch, EMB), F32) + bb_ref[...]
+    features = dense_ref.shape[0]
+    turn[0:features, :] = dense_ref[...]
+    turn[features:features + 1, :] = label_ref[...].astype(F32)
+    dense = turn[...].T
+    label = dense[:, features:features + 1]
+    for j in range(features):
+        bottom = bottom + dense[:, j:j + 1] * bw_ref[j:j + 1, :]
+    base[:, 0:EMB] = jnp.maximum(bottom, 0.0).astype(BF16)
+
+    @pl.loop(0, feats)
+    def _(f):
+        at = pl.ds(pl.multiple_of((f + 1) * EMB, EMB), EMB)
+        base[:, at] = jnp.dot(pick[f], rows[...], preferred_element_type=F32).astype(BF16)
+
+    nt = (((1,), (1,)), ((), ()))
+    low_wide = lax.dot_general(base[...], down_ref[...], nt, preferred_element_type=F32)
+    low = low_wide.astype(BF16)
+    low_t = low.astype(F32).T.astype(BF16)
+    step = width // len(plan)
+    lsum = jnp.zeros((batch, LANES), F32)
+    for c in range(width // step):
+        at = slice(c * step, (c + 1) * step)
+        g = jnp.dot(low, up_ref[:, at], preferred_element_type=F32) + bias_ref[:, at]
+        gate[:, at] = g
+        b = base[:, at].astype(F32)
+        x = (b * g + b) * outw_ref[:, at]
+        for i in range(step // LANES):
+            lsum = lsum + x[:, i * LANES:(i + 1) * LANES]
+    logit = jnp.sum(lsum, axis=1, keepdims=True)
+    lgrad = jax.nn.sigmoid(logit) - label
+
+    for c in range(width // step):
+        at = slice(c * step, (c + 1) * step)
+        gc = lgrad * outw_ref[:, at]
+        gcross[:, at] = (gc * base[:, at].astype(F32)).astype(BF16)
+    g_low = lax.dot_general(gcross[...], up_ref[...], nt, preferred_element_type=F32)
+    g_low = g_low.astype(BF16)
+    g_low_t = g_low.astype(F32).T.astype(BF16)
+    devices, two = acc_ref.shape[0], acc_ref.shape[1]
+    half = two // 2
+    for c, place in enumerate(plan):
+        at = slice(c * step, (c + 1) * step)
+        up = jnp.dot(low_t, gcross[:, at], preferred_element_type=F32)
+        down = jnp.dot(g_low_t, base[:, at], preferred_element_type=F32)
+        for d in range(devices):
+            acc_ref[place[d], 0:half, at] = up[d * half:(d + 1) * half, :]
+            acc_ref[place[d], half:two, at] = down[d * half:(d + 1) * half, :]
+        gc = lgrad * outw_ref[:, at]
+        grad[:, at] = gc * (gate[:, at] + 1.0) + jnp.dot(
+            g_low, down_ref[:, at], preferred_element_type=F32
+        )
+
+    total = jnp.zeros((EMB, cache), F32)
+    for f in range(feats):
+        gp = grad[:, (f + 1) * EMB:(f + 2) * EMB].T.astype(BF16)
+        total = total + jnp.dot(gp, pick[f], preferred_element_type=F32)
+    total = total.T
+    cold_grad[...] = total[:cold].astype(BF16)
+    hot_grad[...] = total[cold:].astype(BF16)
+
+
+def compute(plan, devices, cold, hot, ids, weight, length, dense, labels, up, down, bias, outw, bw, bb):
+    feats, bag, batch = ids.shape
+    padded = -(-feats * bag // LANES) * LANES
+    width = up.shape[1]
+    cache = cold.shape[0] + hot.shape[0]
+    share = up.shape[0] // devices
+    return pl.pallas_call(
+        functools.partial(compute_kernel, plan, bag),
+        out_shape=[
+            jax.ShapeDtypeStruct((devices, 2 * share, width), F32),
+            jax.ShapeDtypeStruct(cold.shape, BF16),
+            jax.ShapeDtypeStruct(hot.shape, BF16),
+        ],
+        in_specs=vmem(13),
+        out_specs=vmem(3),
+        scratch_shapes=[
+            pltpu.VMEM((feats, batch, cache), BF16),
+            pltpu.VMEM((cache, EMB), BF16),
+            pltpu.VMEM((batch, width), BF16),
+            pltpu.VMEM((batch, width), F32),
+            pltpu.VMEM((batch, width), BF16),
+            pltpu.VMEM((batch, width), F32),
+            pltpu.VMEM((batch, padded), F32),
+            pltpu.VMEM((batch, padded), F32),
+            pltpu.VMEM((padded, batch), F32),
+        ],
+        name="compute",
+    )(cold, hot, ids, weight, length, dense, labels, up, down, bias, outw, bw, bb)
+
+
+def reduce_kernel(
+    stages, n_table, n_rep, buffers,
+    acc_in, tg_cold, tg_hot, ask_ref, hot_ref,
+    up_out, down_out, table_out,
+    acc, rc_cold, rc_hot, own_cold, own_hot, ag_cold, ag_hot, own_ids, ag_ids,
+    *rest,
+):
+    sends = rest[:buffers]
+    recvs = rest[buffers:2 * buffers]
+    w_send, w_recv, c_send, c_recv, h_send, h_recv, a_send, a_recv = rest[2 * buffers:]
+    t = lax.axis_index("table")
+    r = lax.axis_index("replica")
+    parts = len(stages)
+    step = acc.shape[2] // parts
+
+    def table_peer(k):
+        return (lax.rem(t + k, n_table), r)
+
+    def rep_peer(k):
+        return (t, lax.rem(r + k, n_rep))
+
+    barrier = pltpu.get_barrier_semaphore()
+    for k in range(1, n_table):
+        pl.semaphore_signal(barrier, inc=1, device_id=table_peer(k), device_id_type=MESH)
+    for k in range(1, n_rep):
+        pl.semaphore_signal(barrier, inc=1, device_id=rep_peer(k), device_id_type=MESH)
+    pl.semaphore_wait(barrier, n_table - 1 + n_rep - 1)
+
+    def bit_of(axis, bit):
+        return lax.rem((t if axis == "table" else r) // (1 << bit), 2)
+
+    def partner(axis, bit):
+        mine = bit_of(axis, bit)
+        shift = (1 - 2 * mine) * (1 << bit)
+        return (t + shift, r) if axis == "table" else (t, r + shift)
+
+    lows = [0] * parts
+    sizes = [acc.shape[0]] * parts
+    copies = {}
+
+    def launch(p, s):
+        axis, bit = stages[p][s]
+        mine = bit_of(axis, bit)
+        half = sizes[p] // 2
+        keep = lows[p] + mine * half
+        give = lows[p] + (1 - mine) * half
+        cols = slice(p * step, (p + 1) * step)
+        i = p * len(stages[p]) + s
+        src = acc_in if s == 0 else acc
+        sends[i][...] = src[pl.ds(give, half), :, cols].astype(BF16)
+        c = pltpu.make_async_remote_copy(
+            src_ref=sends[i], dst_ref=recvs[i], send_sem=w_send.at[i], recv_sem=w_recv.at[i],
+            device_id=partner(axis, bit), device_id_type=MESH,
+        )
+        c.start()
+        copies[p, s] = c
+        lows[p], sizes[p] = keep, half
+
+    def absorb(p, s):
+        copies[p, s].wait()
+        i = p * len(stages[p]) + s
+        cols = slice(p * step, (p + 1) * step)
+        at = pl.ds(lows[p], sizes[p])
+        src = acc_in if s == 0 else acc
+        total = src[at, :, cols] + recvs[i][...].astype(F32)
+        if s + 1 < len(stages[p]):
+            acc[at, :, cols] = total
+        else:
+            half = acc.shape[1] // 2
+            up_out[:, cols] = total[0, 0:half]
+            down_out[:, cols] = total[0, half:]
+
+    cold_copies, hot_copies = [], []
+    for k in range(1, n_table):
+        cold_copies.append(pltpu.make_async_remote_copy(
+            src_ref=tg_cold.at[table_peer(k)[0]], dst_ref=rc_cold.at[t],
+            send_sem=c_send.at[k], recv_sem=c_recv.at[k],
+            device_id=table_peer(k), device_id_type=MESH))
+        hot_copies.append(pltpu.make_async_remote_copy(
+            src_ref=tg_hot.at[:, table_peer(k)[0]], dst_ref=rc_hot.at[t],
+            send_sem=h_send.at[k], recv_sem=h_recv.at[k],
+            device_id=table_peer(k), device_id_type=MESH))
+    for p in range(parts):
+        launch(p, 0)
+    for c in cold_copies + hot_copies:
+        c.start()
+    rc_cold[t] = tg_cold[t]
+    rc_hot[t] = tg_hot[:, t]
+    own_ids[...] = ask_ref[:, :, 0, :]
+    for p in range(parts):
+        absorb(p, 0)
+        launch(p, 1)
+    for c in cold_copies + hot_copies:
+        c.wait()
+    own_cold[...] = rc_cold[...]
+    hot_sum = rc_hot[0].astype(F32)
+    for o in range(1, n_table):
+        hot_sum = hot_sum + rc_hot[o].astype(F32)
+    own_hot[...] = hot_sum
+    back = []
+    for k in range(1, n_rep):
+        for n, (src, dst) in enumerate(
+            ((own_cold, ag_cold), (own_hot, ag_hot), (own_ids, ag_ids))
+        ):
+            back.append(pltpu.make_async_remote_copy(
+                src_ref=src, dst_ref=dst.at[r], send_sem=a_send.at[n, k],
+                recv_sem=a_recv.at[n, k], device_id=rep_peer(k), device_id_type=MESH))
+    for c in back:
+        c.start()
+    ag_cold[r] = own_cold[...]
+    ag_hot[r] = own_hot[...]
+    ag_ids[r] = own_ids[...]
+    deep = len(stages[0])
+    for s in range(1, deep):
+        for p in range(parts):
+            absorb(p, s)
+            if s + 1 < deep:
+                launch(p, s + 1)
+        if s == min(2, deep - 1):
+            for c in back:
+                c.wait()
+            mine = table_out.shape[0]
+            first = r * mine
+            wants = own_ids.shape[1]
+            total = [jnp.zeros((BLOCK, EMB), F32) for _ in range(mine)]
+            for q in range(n_rep):
+                for o in range(n_table):
+                    for w in range(wants):
+                        ids = ag_ids[q, o, w:w + 1, :] - first
+                        val = ag_cold[q, o, w].astype(F32)
+                        for b in range(mine):
+                            total[b] = total[b] + jnp.where(ids == b, val, 0.0)
+            for h in range(hot_ref.shape[0]):
+                ids = hot_ref[h, 0:1, :] - first
+                live = hot_ref[h, 0:1, :] >= 0
+                val = ag_hot[0, h]
+                for q in range(1, n_rep):
+                    val = val + ag_hot[q, h]
+                for b in range(mine):
+                    total[b] = total[b] + jnp.where((ids == b) & live, val, 0.0)
+            for b in range(mine):
+                table_out[b] = total[b]
+
+
+def reduce(stages, n_table, n_rep, block_total, acc, tg_cold, tg_hot, ask, hot_ids):
+    devices, two, width = acc.shape
+    parts = len(stages)
+    step = width // parts
+    slots, wants = hot_ids.shape[0], tg_cold.shape[1]
+    shapes = []
+    for part in stages:
+        size = devices
+        for _ in part:
+            size //= 2
+            shapes.append(pltpu.VMEM((size, two, step), BF16))
+    dma = pltpu.SemaphoreType.DMA
+    return pl.pallas_call(
+        functools.partial(reduce_kernel, stages, n_table, n_rep, len(shapes)),
+        out_shape=[
+            jax.ShapeDtypeStruct((two // 2, width), F32),
+            jax.ShapeDtypeStruct((two // 2, width), F32),
+            jax.ShapeDtypeStruct((block_total // n_rep, BLOCK, EMB), F32),
+        ],
+        in_specs=vmem(5),
+        out_specs=vmem(3),
+        scratch_shapes=[
+            pltpu.VMEM(acc.shape, F32),
+            pltpu.VMEM((n_table, wants, BLOCK, EMB), BF16),
+            pltpu.VMEM((n_table, slots, BLOCK, EMB), BF16),
+            pltpu.VMEM((n_table, wants, BLOCK, EMB), BF16),
+            pltpu.VMEM((slots, BLOCK, EMB), F32),
+            pltpu.VMEM((n_rep, n_table, wants, BLOCK, EMB), BF16),
+            pltpu.VMEM((n_rep, slots, BLOCK, EMB), F32),
+            pltpu.VMEM((n_table, wants, LANES), jnp.int32),
+            pltpu.VMEM((n_rep, n_table, wants, LANES), jnp.int32),
+        ] + shapes + shapes + [
+            dma((len(shapes),)), dma((len(shapes),)),
+            dma((n_table,)), dma((n_table,)), dma((n_table,)), dma((n_table,)),
+            dma((3, n_rep)), dma((3, n_rep)),
+        ],
+        compiler_params=pltpu.CompilerParams(collective_id=1, has_side_effects=True),
+        name="reduce",
+    )(acc, tg_cold, tg_hot, ask, hot_ids)
+
+
+def make_stages(n_table, n_rep, parts):
+    rep = [("replica", b) for b in range(n_rep.bit_length() - 1)]
+    tab = [("table", b) for b in range(n_table.bit_length() - 1)]
+    bits = rep + tab
+    head, tail = bits[:1], bits[1:]
+    return [head + tail[p % len(tail):] + tail[:p % len(tail)] for p in range(parts)]
+
+
+def places(stages, n_rep, devices):
+    plan = []
+    for part in stages:
+        row = []
+        for d in range(devices):
+            at = 0
+            for axis, bit in part:
+                number = d // n_rep if axis == "table" else d % n_rep
+                at = at * 2 + (number >> bit) % 2
+            row.append(at)
+        plan.append(row)
+    return plan
+
+
+def fast_local(
+    emb_table, cross_up, cross_down, cross_bias, out_weight, bottom_weight, bottom_bias,
+    dense_in, labels, lookup_ids, bag_weight, bag_length, want_blocks, hot_blocks, hot_count,
+):
+    owners, reps = lax.axis_size("table"), lax.axis_size("replica")
+    devices = owners * reps
+    wants, slots = want_blocks.shape[3], hot_blocks.shape[1]
+    want = jnp.broadcast_to(
+        want_blocks.reshape(owners, wants)[:, :, None, None], (owners, wants, SUBLANES, LANES)
+    )
+    alive = jnp.arange(slots, dtype=jnp.int32) < hot_count[0]
+    hot_ids = jnp.broadcast_to(
+        jnp.where(alive, hot_blocks[0], -1)[:, None, None], (slots, SUBLANES, LANES)
+    )
+    cold, hot, ask = fetch(want, hot_ids, emb_table, owners)
+    parts = 3
+    stages = make_stages(owners, reps, parts)
+    plan = places(stages, reps, devices)
+    acc, cold_grad, hot_grad = compute(
+        plan, devices, cold.reshape(-1, EMB), hot.reshape(-1, EMB),
+        lookup_ids.transpose(1, 2, 0), bag_weight.transpose(1, 2, 0), bag_length.T,
+        dense_in.T, labels[None],
+        cross_up, cross_down, cross_bias[None], out_weight[None], bottom_weight,
+        bottom_bias[None],
+    )
+    up, down, table = reduce(
+        stages, owners, reps, emb_table.shape[0] // BLOCK, acc, cold_grad.reshape(cold.shape),
+        hot_grad.reshape(hot.shape), ask, hot_ids,
+    )
+    return up, down, table.reshape(-1, EMB)
 
 
 def local_step(
@@ -65,7 +538,7 @@
     return (up_part, down_part, cache_grad)
 
 
-def local(
+def plain_local(
     emb_table,
     cross_up,
     cross_down,
@@ -138,7 +611,21 @@
     return (up_grad, down_grad, table_grad)
 
 
+def choose(mesh, *args):
+    devices = mesh.shape["table"] * mesh.shape["replica"]
+    powers = all(n > 1 and n & (n - 1) == 0 for n in mesh.shape.values())
+    rank, width = args[1].shape
+    ids, want, hot = args[9], args[12], args[13]
+    cache = mesh.shape["table"] * (want.shape[3] + hot.shape[1]) * BLOCK
+    picked = 2 * ids.shape[0] * ids.shape[1] * cache
+    whole_tiles = rank % (devices * SUBLANES) == 0 and width % (3 * LANES) == 0
+    if powers and whole_tiles and picked < 2**23:
+        return fast_local(*args)
+    return plain_local(*args)
+
+
 def solution(mesh):
+    local = functools.partial(choose, mesh)
     placed = (
         P("table", None),
         P(),

time: 506 us -> 83.1 us (0.16)
  waiting for transfers between devices: 253 us -> 0 us
  other arithmetic: 88.5 us -> 0.66 us
  local copies, waits for them, and re-layouts: 87.6 us -> 9.33 us
  Pallas kernels: 0 us -> 71.5 us
  blocking collectives: 31.3 us -> 0 us
  starting transfers between devices: 18.7 us -> 0 us
  between operations: 14.7 us -> 1.3 us
  matrix products: 11.4 us -> 0 us
    unnamed x5 -> x0, waiting for transfers between devices: 223 us -> none
    scatter-add x1 -> x0, other arithmetic: 78.3 us -> none  [local_step(): cache_grad = jnp.zeros(cached_rows.shape, jnp.float32).at[ids_dev.reshape...]
    pallas_call x0 -> x3, Pallas kernels: none -> 71.5 us  [the longest x1 34.5 us: reduce(): pl.pallas_call(functools.partial(reduce_kernel, stages, n_table, n_rep, l...]
    gather x3 -> x0, local copies, waits for them, and re-layouts: 50.4 us -> none  [the longest x1 46.8 us: local_step(): gathered = cached_rows[ids_dev].astype(jnp.float32)]
    all_gather x1 -> x0, blocking collectives: 31.3 us -> none  [local(): hot_rows = lax.all_gather(own_hot[:, None], 'table', axis=1, tiled=True)]
    reduce_scatter x1 -> x0, waiting for transfers between devices: 23.2 us -> none  [local(): lax.psum_scatter(block_grad.reshape(-1, EMB), 'replica', scatter_dimensio...]
    all_to_all x3 -> x0, starting transfers between devices: 18.6 us -> none  [the longest x1 7.28 us: local(): lax.all_to_all(wanted, 'table', split_axis=0, concat_axis=0, tiled=True)]
    mul x3 -> x0, local copies, waits for them, and re-layouts: 11.5 us -> none  [the longest x2 8.82 us: local_step(): contrib = bag_coef[..., None] * grad_pooled[:, :, None, :]]
  transfers between devices with their start and end apart: 6 -> 0, of which waited for: 4 -> 0; matrix products, arithmetic and copies ran while one was open for 6% -> 0% of each run, Pallas kernels for 0% -> 0%
where the time goes in v1:
time: 83.1 us; the launch traced here: 82.8 us
  Pallas kernels  71.5 us (86%)
  local copies, waits for them, and re-layouts  9.33 us (11%)
  between operations  1.3 us (2%)
    pallas_call x1, Pallas kernels, reduce(): pl.pallas_call(functools.partial(reduce_kernel, stages, n_table, n_rep, l...  34.5 us
    pallas_call x1, Pallas kernels, compute(): pl.pallas_call(functools.partial(compute_kernel, plan, bag), out_shape=[j...  20.2 us
    pallas_call x1, Pallas kernels, fetch(): pl.pallas_call(functools.partial(fetch_kernel, owners), out_shape=[jax.Sh...  16.8 us
    unnamed x3, local copies, waits for them, and re-layouts  4.66 us

profile of v1, /device:TPU:0, one launch (start us, length us, event | category | flops | bytes accessed | tf_op | source)
XLA Modules:
  0.0 82.8 jit_solution(17110313533576415031)
XLA Ops:
  1.3 0.7 compare_select_fusion
  1.9 0.7 broadcast_in_dim.32.hot_ref
  2.6 1.3 %broadcast_in_dim.34.bias_ref = f32[1,3456]{1,0:T(1,128)} reshape(f32[3456]{0:T(1024)} %param.18) | data formatting | bytes 27648 | tf_op jit(solution)/shard_map/broadcast_in_dim | solution.py:473
  3.9 1.3 %broadcast_in_dim.35.outw_ref = f32[1,3456]{1,0:T(1,128)} reshape(f32[3456]{0:T(1024)} %param.19) | data formatting | bytes 27648 | tf_op jit(solution)/shard_map/broadcast_in_dim | solution.py:473
  5.3 1.3 %broadcast_in_dim.30.want_ref = s32[8,1,8,128]{3,2,1,0:T(8,128)} broadcast(s32[8]{0:T(128)} %bitcast.25), dimensions={0} | broadcast | bytes 32800 | tf_op jit(solution)/shard_map/broadcast_in_dim | solution.py:458
  6.6 16.8 %fetch.1 = (bf16[8,1,32,128]{3,2,1,0:T(8,128)(2,1)}, bf16[2,8,32,128]{3,2,1,0:T(8,128)(2,1)}, s32[8,1,8,128]{3,2,1,0:T(8,128)}) custom-call(s32[8,1,8,128]{3,2,1,0:T(8,128)} %broadcast_in_dim.30.want_ref, s32[2,8,128]{2,1,0:T(8,128)} %broadcast_in_dim.32.hot_ref, bf16[1024,128]{1,0:T(8,128)(2,1)} %emb_ref.1), custom_call_target="tpu_custom_call" | custom-call | tf_op jit(solution)/shard_map/fetch/pallas_call | solution.py:96
  23.4 20.2 %compute.1 = (f32[32,16,3456]{2,1,0:T(8,128)}, bf16[256,128]{1,0:T(8,128)(2,1)}, bf16[512,128]{1,0:T(8,128)(2,1)}) custom-call(bf16[256,128]{1,0:T(8,128)(2,1)} %bitcast.20, bf16[512,128]{1,0:T(8,128)(2,1)} %bitcast.17, s32[26,4,128]{2,1,0:T(4,128)} %bitcast.21, f32[26,4,128]{2,1,0:T(4,128)} %bitcast.22, s32[26,128]{1,0:T(8,128)} %bitcast.23, ...), custom_call_target="tpu_custom_call" | custom-call | tf_op jit(solution)/shard_map/compute/pallas_call | solution.py:220
  43.6 34.5 %reduce.1 = (f32[8,3456]{1,0:T(8,128)}, f32[8,3456]{1,0:T(8,128)}, f32[8,32,128]{2,1,0:T(8,128)}) custom-call(f32[32,16,3456]{2,1,0:T(8,128)} %get-tuple-element.14.acc_in, bf16[8,1,32,128]{3,2,1,0:T(8,128)(2,1)} %bitcast.19, bf16[2,8,32,128]{3,2,1,0:T(8,128)(2,1)} %bitcast.16, s32[8,1,8,128]{3,2,1,0:T(8,128)} %get-tuple-element.17.ask_ref, ...), custom_call_target="tpu_custom_call" | custom-call | tf_op jit(solution)/shard_map/reduce/pallas_call | solution.py:400
  78.1 1.5 %copy.22 = f32[8,3456]{1,0:T(8,128)} copy(f32[8,3456]{1,0:T(8,128)} %get-tuple-element.24) | data formatting | bytes 221184
  79.7 1.5 %copy.23 = f32[8,3456]{1,0:T(8,128)} copy(f32[8,3456]{1,0:T(8,128)} %get-tuple-element.25) | data formatting | bytes 221184
  81.2 1.6 %copy.24 = f32[256,128]{1,0:T(8,128)} copy(f32[256,128]{1,0:T(8,128)} %bitcast.18) | data formatting | bytes 262144
